TPU v7x, 256 devices: a whole 4x4x8 slice. The times are simulated.
256 devices in a mesh: grid: 64 (over z, y, core), snap: 4 (over x).
Axes of the slice: x: 4, y: 4, z: 8, core: 2. Of those that a mesh axis runs over, the one named last changes fastest.
Arguments:
- fields: bfloat16 [393216, 1024], P('grid', 'snap'), may hold values from -40 to 40
- start_local: float32 [1024, 128], P('snap'), may hold values from -6 to 6
- start_pair: float32 [2, 256, 128], replicated, may hold values from -6 to 6
- start_root: float32 [256, 128], replicated, may hold values from -6 to 6
Outputs:
- modes: bfloat16 [393216, 128], P(('grid', 'snap'))
All inputs are finite; a program needn't handle non-finite values.
Results may differ from a plain program's by a relative error of at most 0.0055.
Values may be sent and summed in bfloat16 or wider, within the bound.
A program may use at most 64 MiB of HBM per device.

v0:
```python
import functools

import jax
import jax.numpy as jnp
from jax import lax
from jax.experimental import pallas as pl
from jax.experimental.pallas import tpu as pltpu
from jax.sharding import Mesh
from jax.sharding import PartitionSpec as P

POWER = 2
NEWTON = 8
RANK = 128
NZ, NY, NC, NX = 8, 4, 2, 4
ROW = NY * NC
SHEET = NZ * NY
PLANE = NX * ROW
EARLY = 3
PIECE = 384
MESH = pl.DeviceIdType.MESH
F32 = jnp.float32
BF16 = jnp.bfloat16


def product(a, b):
    return jnp.dot(a, b, preferred_element_type=F32)


def product_t(a, b):
    return lax.dot_general(a, b, (((0,), (0,)), ((), ())), preferred_element_type=F32)


def halves(a):
    high = a.astype(BF16)
    return high, (a - high.astype(F32)).astype(BF16)


def three_products(a, b, dims):
    (a_high, a_low), (b_high, b_low) = halves(a), halves(b)
    (a_dim,), (b_dim,) = dims
    left = jnp.concatenate([a_high, a_high, a_low], axis=a_dim)
    right = jnp.concatenate([b_high, b_low, b_high], axis=b_dim)
    return lax.dot_general(left, right, (dims, ((), ())), preferred_element_type=F32)


def power_steps(grams, bases):
    steps = [three_products(basis, gram, ((1,), (0,))) for gram, basis in zip(grams, bases)]
    flat = [w * (1.0 / jnp.sqrt(jnp.sum(w * w) + 1e-06)) for w in steps]
    for _ in range(NEWTON):
        inner = [three_products(w, w, ((1,), (1,))) for w in flat]
        flat = [1.5 * w - 0.5 * three_products(s, w, ((1,), (0,))) for s, w in zip(inner, flat)]
    return flat


def turned(gram, left, right):
    high, low = halves(gram)
    middle = product(jnp.concatenate([high, low], axis=1), jnp.concatenate([right, right], axis=0))
    high, low = halves(middle)
    return product_t(jnp.concatenate([left, left], axis=0), jnp.concatenate([high, low], axis=0))


def body(
    inverse_count,
    fields, start_local, start_pair, start_root,
    out,
    f, s_local, s_pair, s_root,
    gram, got_c, part_a, got_a, mine_a, col,
    raw, rot_all, leaves, sent_leaf, diag, diag_part, diag_all,
    pair_part, got_p, mine_p, zs_p, pair_all, piece_p,
    cross_part, got_x, mine_x, zs_x, cross_all, piece_x,
    load_sem, start_sem, c_sem, a_sem, b_sem, d_sem, raw_sem, rot_sem, leaf_sem, e_sem, g_sem, p_sem, x_sem,
):
    z, y, c, x = (lax.axis_index(name) for name in ("z", "y", "c", "x"))
    j = y * NC + c
    m = z * NY + y
    t = x * ROW + j
    quarter = f.shape[0] // NX
    early = raw.shape[1]
    late = quarter - early
    pending = []

    def send(src, dst, sems, **where):
        pltpu.make_async_remote_copy(
            src_ref=src, dst_ref=dst, send_sem=sems.at[0], recv_sem=sems.at[1],
            device_id=where, device_id_type=MESH,
        ).start()

    def await_bytes(ref, sem):
        pltpu.make_async_copy(ref, ref, sem).wait()

    def arrived(ref, sems):
        pending.append((ref, sems.at[0]))
        await_bytes(ref, sems.at[1])

    def greet(**where):
        pl.semaphore_signal(pltpu.get_barrier_semaphore(), inc=1, device_id=where, device_id_type=MESH)

    def in_row(d):
        peer = lax.rem(j + d, ROW)
        return peer, dict(y=peer // NC, c=lax.rem(peer, NC))

    def in_sheet(d):
        peer = lax.rem(m + d, SHEET)
        return peer, dict(z=peer // NY, y=lax.rem(peer, NY))

    def in_plane(d):
        peer = lax.rem(t + d, PLANE)
        return peer, dict(x=peer // ROW, y=lax.rem(peer // NC, NY), c=lax.rem(peer, NC))

    loads = []
    for k in range(NX):
        rows = pl.ds(k * quarter, quarter)
        loads.append(pltpu.make_async_copy(fields.at[rows], f.at[rows], load_sem.at[k]))
    own_early = pl.ds(pl.multiple_of(x * quarter, quarter), early)
    loads.append(pltpu.make_async_copy(fields.at[own_early], raw.at[x], load_sem.at[NX]))
    for k, (src, dst) in enumerate([(start_local, s_local), (start_pair, s_pair), (start_root, s_root)]):
        loads.append(pltpu.make_async_copy(src, dst, start_sem.at[k]))
    for load in loads:
        load.start()

    @pl.loop(1, SHEET)
    def _(d):
        greet(**in_sheet(d)[1])

    greet(c=1 - c)
    for d in range(1, NX):
        greet(x=lax.rem(x + d, NX))

    total = None
    for k in range(NX):
        loads[k].wait()
        part = f[pl.ds(k * quarter, quarter)]
        term = product_t(part, part)
        total = term if total is None else total + term
    gram[...] = total
    pl.semaphore_wait(pltpu.get_barrier_semaphore(), SHEET - 1 + 1 + NX - 1)

    half = gram.shape[0] // NC
    send(gram.at[pl.ds(pl.multiple_of((1 - c) * half, 8), half)], got_c, c_sem, c=1 - c)

    @pl.loop(0, early // PIECE)
    def _(k):
        for d in (2, 1, 3):
            peer = lax.rem(x + d, NX)
            rows = pl.ds(pl.multiple_of(peer * quarter + k * PIECE, PIECE), PIECE)
            send(f.at[rows], raw.at[x, pl.ds(pl.multiple_of(k * PIECE, PIECE), PIECE)], raw_sem, x=peer)

    arrived(got_c, c_sem)
    kept = gram[pl.ds(pl.multiple_of(c * half, 8), half)] + got_c[...]
    for n in range(SHEET):
        r, s = 8 * (n // 2), 128 * (n % 2)
        part_a[n] = kept[r:r + 8, s:s + 128]

    @pl.loop(1, SHEET)
    def _(d):
        peer, where = in_sheet(d)
        send(part_a.at[peer], got_a.at[d - 1], a_sem, **where)

    arrived(got_a, a_sem)
    tile = (part_a[m] + got_a[...].sum(axis=0)) * inverse_count
    mine_a[...] = tile
    col[c, m] = tile

    @pl.loop(1, SHEET)
    def _(d):
        send(mine_a, col.at[c, m], b_sem, **in_sheet(d)[1])

    arrived(col.at[0, pl.ds(0, SHEET - 1)], b_sem)
    send(col.at[c], col.at[c], d_sem, c=1 - c)
    arrived(col.at[0], d_sem)
    whole = jnp.concatenate(
        [
            jnp.concatenate([col[n, 2 * k], col[n, 2 * k + 1]], axis=1)
            for n in range(NC)
            for k in range(SHEET // 2)
        ],
        axis=0,
    )
    for load in loads[NX:]:
        load.wait()
    bases = [s_local[...].T]
    for _ in range(POWER):
        bases = power_steps([whole], bases)
    rotation = bases[0].T.astype(BF16)

    rot_all[x] = rotation
    for d in (2, 1, 3):
        send(rot_all.at[x], rot_all.at[x], rot_sem, x=lax.rem(x + d, NX))
    for n, d in enumerate((2, 1, 3)):
        peer = lax.rem(x + d, NX)
        rows = pl.ds(pl.multiple_of(peer * quarter + early, PIECE), late)
        sent_leaf[n] = product(f[rows], rotation).astype(BF16)
        send(sent_leaf.at[n], leaves.at[x, pl.ds(early, late)], leaf_sem, x=peer)

    diag[...] = turned(whole, rotation, rotation)
    part16 = pl.ds(pl.multiple_of(j * 16, 16), 16)
    diag_part[x] = diag[part16]
    for d in (1, 2, 3):
        send(diag.at[part16], diag_part.at[x], e_sem, x=lax.rem(x + d, NX))

    own_late = pl.ds(pl.multiple_of(x * quarter + early, PIECE), late)
    leaves[x, pl.ds(early, late)] = product(f[own_late], rotation).astype(BF16)

    arrived(raw.at[pl.ds(0, NX - 1)], raw_sem)
    arrived(rot_all.at[pl.ds(0, NX - 1)], rot_sem)
    for b in range(NX):
        leaves[b, pl.ds(0, early)] = product(raw[b], rot_all[b]).astype(BF16)
    arrived(leaves.at[pl.ds(0, NX - 1), pl.ds(early, late)], leaf_sem)

    pair_part[0:128] = product_t(leaves[0], leaves[1])
    pair_part[128:256] = product_t(leaves[2], leaves[3])

    @pl.loop(1, PLANE)
    def _(d):
        peer, where = in_plane(d)
        send(pair_part.at[pl.ds(pl.multiple_of(peer * 8, 8), 8)], got_p.at[d - 1], p_sem.at[0], **where)

    left = jnp.concatenate([leaves[0], leaves[1]], axis=1)
    right = jnp.concatenate([leaves[2], leaves[3]], axis=1)
    cross_part[...] = product_t(left, right)

    @pl.loop(1, PLANE)
    def _(d):
        peer, where = in_plane(d)
        send(cross_part.at[pl.ds(pl.multiple_of(peer * 8, 8), 8)], got_x.at[d - 1], x_sem.at[0], **where)

    arrived(diag_part.at[pl.ds(0, NX - 1)], e_sem)
    diag_all[j] = diag_part[...]

    @pl.loop(1, ROW)
    def _(d):
        send(diag_part, diag_all.at[j], g_sem, **in_row(d)[1])

    my8 = pl.ds(pl.multiple_of(t * 8, 8), 8)

    def over_z(got, part, mine, zs, sems):
        arrived(got, sems.at[0])
        value = part[my8] + got[...].sum(axis=0)
        mine[...] = value
        zs[z] = value

        @pl.loop(1, NZ)
        def _(d):
            send(mine, zs.at[z], sems.at[1], z=lax.rem(z + d, NZ))

    def to_plane(zs, piece, whole_ref, sems):
        arrived(zs.at[pl.ds(0, NZ - 1)], sems.at[1])
        value = zs[...].sum(axis=0) * inverse_count
        piece[...] = value
        whole_ref[my8] = value

        @pl.loop(1, PLANE)
        def _(d):
            send(piece, whole_ref.at[my8], sems.at[2], **in_plane(d)[1])

    def from_plane(whole_ref, sems):
        arrived(whole_ref.at[pl.ds(0, 8 * (PLANE - 1))], sems.at[2])

    over_z(got_p, pair_part, mine_p, zs_p, p_sem)
    to_plane(zs_p, piece_p, pair_all, p_sem)
    over_z(got_x, cross_part, mine_x, zs_x, x_sem)
    arrived(diag_all.at[pl.ds(0, ROW - 1)], g_sem)
    diags = [jnp.concatenate([diag_all[n, b] for n in range(ROW)], axis=0) for b in range(NX)]
    from_plane(pair_all, p_sem)

    def pair_gram(n):
        block = pair_all[128 * n:128 * n + 128]
        top = jnp.concatenate([diags[2 * n], block], axis=1)
        low = jnp.concatenate([block.T, diags[2 * n + 1]], axis=1)
        return jnp.concatenate([top, low], axis=0)

    grams = [pair_gram(0), pair_gram(1)]
    bases = power_steps(grams, [s_pair[n].T for n in range(2)])
    to_plane(zs_x, piece_x, cross_all, x_sem)
    bases = power_steps(grams, bases)
    rotations = [basis.T.astype(BF16) for basis in bases]
    first = turned(grams[0], rotations[0], rotations[0])
    second = turned(grams[1], rotations[1], rotations[1])
    from_plane(cross_all, x_sem)
    mixed = turned(cross_all[...], rotations[0], rotations[1])
    root_gram = jnp.concatenate(
        [jnp.concatenate([first, mixed], axis=1), jnp.concatenate([mixed.T, second], axis=1)], axis=0
    )
    bases = [s_root[...].T]
    for _ in range(POWER):
        bases = power_steps([root_gram], bases)
    branch = jnp.concatenate(
        [product(left, rotations[0]).astype(BF16), product(right, rotations[1]).astype(BF16)], axis=1
    )
    out[...] = product(branch, bases[0].T.astype(BF16)).astype(BF16)

    for ref, sem in pending:
        await_bytes(ref, sem)


def on_device(points, fields, start_local, start_pair, start_root):
    rows, snaps = fields.shape
    vmem = pltpu.VMEM
    dma = pltpu.SemaphoreType.DMA
    quarter = rows // NX
    early = EARLY * quarter // 4
    scratch = [
        vmem((rows, snaps), BF16), vmem(start_local.shape, F32), vmem(start_pair.shape, F32), vmem(start_root.shape, F32),
        vmem((snaps, snaps), F32), vmem((snaps // NC, snaps), F32), vmem((SHEET, 8, 128), F32),
        vmem((SHEET - 1, 8, 128), F32), vmem((8, 128), F32), vmem((NC, SHEET, 8, 128), F32),
        vmem((NX, early, snaps), BF16), vmem((NX, snaps, RANK), BF16),
        vmem((NX, quarter, RANK), BF16), vmem((NX - 1, quarter - early, RANK), BF16), vmem((RANK, RANK), F32),
        vmem((NX, 16, RANK), F32), vmem((ROW, NX, 16, RANK), F32),
        vmem((256, 128), F32), vmem((PLANE - 1, 8, 128), F32), vmem((8, 128), F32), vmem((NZ, 8, 128), F32),
        vmem((256, 128), F32), vmem((8, 128), F32),
        vmem((256, 256), F32), vmem((PLANE - 1, 8, 256), F32), vmem((8, 256), F32), vmem((NZ, 8, 256), F32),
        vmem((256, 256), F32), vmem((8, 256), F32),
        dma((NX + 1,)), dma((3,)), *[dma((2,))] * 9, dma((3, 2)), dma((3, 2)),
    ]
    anywhere = pl.BlockSpec(memory_space=pltpu.HBM)
    return pl.pallas_call(
        functools.partial(body, 1.0 / points),
        out_shape=jax.ShapeDtypeStruct((quarter, RANK), BF16),
        in_specs=[anywhere] * 4,
        out_specs=pl.BlockSpec(memory_space=pltpu.VMEM),
        scratch_shapes=scratch,
        compiler_params=pltpu.CompilerParams(
            collective_id=0, has_side_effects=True, vmem_limit_bytes=60 * 2**20
        ),
        name="snapshot_modes",
    )(fields, start_local, start_pair, start_root)


def solution(mesh):
    split = Mesh(mesh.devices.reshape(NZ, NY, NC, mesh.shape["snap"]), ("z", "y", "c", "x"))
    grid = ("z", "y", "c")

    def whole(fields, start_local, start_pair, start_root):
        return jax.shard_map(
            functools.partial(on_device, fields.shape[0]),
            mesh=split,
            in_specs=(P(grid, "x"), P("x", None), P(), P()),
            out_specs=P((*grid, "x"), None),
            check_vma=False,
        )(fields, start_local, start_pair, start_root)

    return whole
```

profile of v0, /device:TPU:1, one launch (start us, length us, event | category | flops | bytes accessed | tf_op | source)
XLA Modules:
  0.0 82.4 jit_solution(15777444197118028247)
XLA Ops:
  0.0 80.6 %snapshot_modes.1 = bf16[1536,128]{1,0:T(8,128)(2,1)} custom-call(bf16[6144,256]{1,0:T(8,128)(2,1)} %fields.1, f32[256,128]{1,0:T(8,128)} %start_local.1, f32[2,256,128]{2,1,0:T(8,128)} %start_pair.1, f32[256,128]{1,0:T(8,128)} %start_root.1), custom_call_target="tpu_custom_call" | custom-call | tf_op jit(solution)/shard_map/snapshot_modes/pallas_call | solution.py:316
  80.7 1.8 %copy.6 = bf16[1536,128]{1,0:T(8,128)(2,1)} copy(bf16[1536,128]{1,0:T(8,128)(2,1)} %snapshot_modes.1) | data formatting | bytes 786432
where the time goes:
time: 82.5 us; the launch traced here: 82.4 us
  Pallas kernels  80.6 us (98%)
  local copies, waits for them, and re-layouts  1.77 us (2%)
    pallas_call x1, Pallas kernels, on_device(): pl.pallas_call(functools.partial(body, 1.0 / points), out_shape=jax.Shape...  80.6 us
    unnamed x1, local copies, waits for them, and re-layouts  1.77 us

commit v1 on v0

--- a/solution.py
+++ b/solution.py
@@ -15,8 +15,8 @@
 ROW = NY * NC
 SHEET = NZ * NY
 PLANE = NX * ROW
-EARLY = 3
-PIECE = 384
+EARLY = 6
+PIECE = 192
 MESH = pl.DeviceIdType.MESH
 F32 = jnp.float32
 BF16 = jnp.bfloat16
@@ -64,15 +64,15 @@
     fields, start_local, start_pair, start_root,
     out,
     f, s_local, s_pair, s_root,
-    gram, got_c, part_a, got_a, mine_a, col,
+    gram, got_c, kept_y, got_y, part_a, got_a, mine_a, col,
     raw, rot_all, leaves, sent_leaf, diag, diag_part, diag_all,
     pair_part, got_p, mine_p, zs_p, pair_all, piece_p,
     cross_part, got_x, mine_x, zs_x, cross_all, piece_x,
-    load_sem, start_sem, c_sem, a_sem, b_sem, d_sem, raw_sem, rot_sem, leaf_sem, e_sem, g_sem, p_sem, x_sem,
+    load_sem, start_sem, near, far, c_sem, y_sem, a_sem, b_sem, d_sem, raw_sem, rot_sem, leaf_sem, e_sem, g_sem, p_sem, x_sem,
 ):
     z, y, c, x = (lax.axis_index(name) for name in ("z", "y", "c", "x"))
     j = y * NC + c
-    m = z * NY + y
+    m = y * NZ + z
     t = x * ROW + j
     quarter = f.shape[0] // NX
     early = raw.shape[1]
@@ -95,17 +95,21 @@
     def greet(**where):
         pl.semaphore_signal(pltpu.get_barrier_semaphore(), inc=1, device_id=where, device_id_type=MESH)
 
-    def in_row(d):
-        peer = lax.rem(j + d, ROW)
-        return peer, dict(y=peer // NC, c=lax.rem(peer, NC))
-
-    def in_sheet(d):
-        peer = lax.rem(m + d, SHEET)
-        return peer, dict(z=peer // NY, y=lax.rem(peer, NY))
-
-    def in_plane(d):
-        peer = lax.rem(t + d, PLANE)
-        return peer, dict(x=peer // ROW, y=lax.rem(peer // NC, NY), c=lax.rem(peer, NC))
+    def away(index, k, size):
+        step = (k + 1) // 2
+        return lax.rem(index + size // 2 + jnp.where(lax.rem(k, 2) == 1, size - step, step), size)
+
+    def in_row(k):
+        peer_y, peer_c = away(y, k // NC, NY), away(c, lax.rem(k, NC), NC)
+        return peer_y * NC + peer_c, dict(y=peer_y, c=peer_c)
+
+    def in_sheet(k):
+        return dict(z=away(z, k // NY, NZ), y=away(y, lax.rem(k, NY), NY))
+
+    def in_plane(k):
+        peer_x = away(x, k // ROW, NX)
+        peer, where = in_row(lax.rem(k, ROW))
+        return peer_x * ROW + peer, dict(x=peer_x, **where)
 
     loads = []
     for k in range(NX):
@@ -118,13 +122,18 @@
     for load in loads:
         load.start()
 
-    @pl.loop(1, SHEET)
-    def _(d):
-        greet(**in_sheet(d)[1])
-
-    greet(c=1 - c)
-    for d in range(1, NX):
-        greet(x=lax.rem(x + d, NX))
+    for k in range(NX - 1):
+        greet(x=away(x, k, NX), c=0)
+    for k in range(NY - 1):
+        greet(y=away(y, k, NY), c=0)
+
+    @pl.when(c == 1)
+    def _():
+        greet(c=0)
+
+    @pl.loop(0, NZ - 1)
+    def _(k):
+        greet(z=away(z, k, NZ), c=1)
 
     total = None
     for k in range(NX):
@@ -133,7 +142,15 @@
         term = product_t(part, part)
         total = term if total is None else total + term
     gram[...] = total
-    pl.semaphore_wait(pltpu.get_barrier_semaphore(), SHEET - 1 + 1 + NX - 1)
+
+    @pl.when(c == 0)
+    def _():
+        pl.semaphore_wait(pltpu.get_barrier_semaphore(), NC * (NX - 1 + NY - 1) + 1)
+        pl.semaphore_signal(near, inc=1, device_id=dict(c=1), device_id_type=MESH)
+
+    @pl.when(c == 1)
+    def _():
+        pl.semaphore_wait(near, 1)
 
     half = gram.shape[0] // NC
     send(gram.at[pl.ds(pl.multiple_of((1 - c) * half, 8), half)], got_c, c_sem, c=1 - c)
@@ -147,23 +164,40 @@
 
     arrived(got_c, c_sem)
     kept = gram[pl.ds(pl.multiple_of(c * half, 8), half)] + got_c[...]
-    for n in range(SHEET):
+    kept_y[...] = kept
+
+    strip = half // NY
+    for k in range(NY - 1):
+        peer = away(y, k, NY)
+        send(kept_y.at[pl.ds(pl.multiple_of(peer * strip, 8), strip)], got_y.at[k], y_sem, y=peer)
+    arrived(got_y, y_sem)
+    sums = kept_y[pl.ds(pl.multiple_of(y * strip, 8), strip)] + got_y[...].sum(axis=0)
+    for n in range(NZ):
         r, s = 8 * (n // 2), 128 * (n % 2)
-        part_a[n] = kept[r:r + 8, s:s + 128]
-
-    @pl.loop(1, SHEET)
-    def _(d):
-        peer, where = in_sheet(d)
-        send(part_a.at[peer], got_a.at[d - 1], a_sem, **where)
+        part_a[n] = sums[r:r + 8, s:s + 128]
+
+    @pl.when(c == 1)
+    def _():
+        pl.semaphore_wait(pltpu.get_barrier_semaphore(), NC * (NZ - 1))
+        pl.semaphore_signal(far, inc=1, device_id=dict(c=0), device_id_type=MESH)
+
+    @pl.when(c == 0)
+    def _():
+        pl.semaphore_wait(far, 1)
+
+    @pl.loop(0, NZ - 1)
+    def _(k):
+        peer = away(z, k, NZ)
+        send(part_a.at[peer], got_a.at[k], a_sem, z=peer)
 
     arrived(got_a, a_sem)
-    tile = (part_a[m] + got_a[...].sum(axis=0)) * inverse_count
+    tile = (part_a[z] + got_a[...].sum(axis=0)) * inverse_count
     mine_a[...] = tile
     col[c, m] = tile
 
-    @pl.loop(1, SHEET)
+    @pl.loop(0, SHEET - 1)
     def _(d):
-        send(mine_a, col.at[c, m], b_sem, **in_sheet(d)[1])
+        send(mine_a, col.at[c, m], b_sem, **in_sheet(d))
 
     arrived(col.at[0, pl.ds(0, SHEET - 1)], b_sem)
     send(col.at[c], col.at[c], d_sem, c=1 - c)
@@ -210,24 +244,24 @@
     pair_part[0:128] = product_t(leaves[0], leaves[1])
     pair_part[128:256] = product_t(leaves[2], leaves[3])
 
-    @pl.loop(1, PLANE)
+    @pl.loop(0, PLANE - 1)
     def _(d):
         peer, where = in_plane(d)
-        send(pair_part.at[pl.ds(pl.multiple_of(peer * 8, 8), 8)], got_p.at[d - 1], p_sem.at[0], **where)
+        send(pair_part.at[pl.ds(pl.multiple_of(peer * 8, 8), 8)], got_p.at[d], p_sem.at[0], **where)
 
     left = jnp.concatenate([leaves[0], leaves[1]], axis=1)
     right = jnp.concatenate([leaves[2], leaves[3]], axis=1)
     cross_part[...] = product_t(left, right)
 
-    @pl.loop(1, PLANE)
+    @pl.loop(0, PLANE - 1)
     def _(d):
         peer, where = in_plane(d)
-        send(cross_part.at[pl.ds(pl.multiple_of(peer * 8, 8), 8)], got_x.at[d - 1], x_sem.at[0], **where)
+        send(cross_part.at[pl.ds(pl.multiple_of(peer * 8, 8), 8)], got_x.at[d], x_sem.at[0], **where)
 
     arrived(diag_part.at[pl.ds(0, NX - 1)], e_sem)
     diag_all[j] = diag_part[...]
 
-    @pl.loop(1, ROW)
+    @pl.loop(0, ROW - 1)
     def _(d):
         send(diag_part, diag_all.at[j], g_sem, **in_row(d)[1])
 
@@ -239,9 +273,9 @@
         mine[...] = value
         zs[z] = value
 
-        @pl.loop(1, NZ)
+        @pl.loop(0, NZ - 1)
         def _(d):
-            send(mine, zs.at[z], sems.at[1], z=lax.rem(z + d, NZ))
+            send(mine, zs.at[z], sems.at[1], z=away(z, d, NZ))
 
     def to_plane(zs, piece, whole_ref, sems):
         arrived(zs.at[pl.ds(0, NZ - 1)], sems.at[1])
@@ -249,7 +283,7 @@
         piece[...] = value
         whole_ref[my8] = value
 
-        @pl.loop(1, PLANE)
+        @pl.loop(0, PLANE - 1)
         def _(d):
             send(piece, whole_ref.at[my8], sems.at[2], **in_plane(d)[1])
 
@@ -281,12 +315,12 @@
     root_gram = jnp.concatenate(
         [jnp.concatenate([first, mixed], axis=1), jnp.concatenate([mixed.T, second], axis=1)], axis=0
     )
+    branch = jnp.concatenate(
+        [product(left, rotations[0]).astype(BF16), product(right, rotations[1]).astype(BF16)], axis=1
+    )
     bases = [s_root[...].T]
     for _ in range(POWER):
         bases = power_steps([root_gram], bases)
-    branch = jnp.concatenate(
-        [product(left, rotations[0]).astype(BF16), product(right, rotations[1]).astype(BF16)], axis=1
-    )
     out[...] = product(branch, bases[0].T.astype(BF16)).astype(BF16)
 
     for ref, sem in pending:
@@ -298,11 +332,11 @@
     vmem = pltpu.VMEM
     dma = pltpu.SemaphoreType.DMA
     quarter = rows // NX
-    early = EARLY * quarter // 4
+    early = EARLY * quarter // 8
     scratch = [
         vmem((rows, snaps), BF16), vmem(start_local.shape, F32), vmem(start_pair.shape, F32), vmem(start_root.shape, F32),
-        vmem((snaps, snaps), F32), vmem((snaps // NC, snaps), F32), vmem((SHEET, 8, 128), F32),
-        vmem((SHEET - 1, 8, 128), F32), vmem((8, 128), F32), vmem((NC, SHEET, 8, 128), F32),
+        vmem((snaps, snaps), F32), vmem((snaps // NC, snaps), F32), vmem((snaps // NC, snaps), F32),
+        vmem((NY - 1, snaps // NC // NY, snaps), F32), vmem((NZ, 8, 128), F32), vmem((NZ - 1, 8, 128), F32), vmem((8, 128), F32), vmem((NC, SHEET, 8, 128), F32),
         vmem((NX, early, snaps), BF16), vmem((NX, snaps, RANK), BF16),
         vmem((NX, quarter, RANK), BF16), vmem((NX - 1, quarter - early, RANK), BF16), vmem((RANK, RANK), F32),
         vmem((NX, 16, RANK), F32), vmem((ROW, NX, 16, RANK), F32),
@@ -310,7 +344,7 @@
         vmem((256, 128), F32), vmem((8, 128), F32),
         vmem((256, 256), F32), vmem((PLANE - 1, 8, 256), F32), vmem((8, 256), F32), vmem((NZ, 8, 256), F32),
         vmem((256, 256), F32), vmem((8, 256), F32),
-        dma((NX + 1,)), dma((3,)), *[dma((2,))] * 9, dma((3, 2)), dma((3, 2)),
+        dma((NX + 1,)), dma((3,)), *[pltpu.SemaphoreType.REGULAR] * 2, *[dma((2,))] * 10, dma((3, 2)), dma((3, 2)),
     ]
     anywhere = pl.BlockSpec(memory_space=pltpu.HBM)
     return pl.pallas_call(
@@ -320,10 +354,10 @@
         out_specs=pl.BlockSpec(memory_space=pltpu.VMEM),
         scratch_shapes=scratch,
         compiler_params=pltpu.CompilerParams(
-            collective_id=0, has_side_effects=True, vmem_limit_bytes=60 * 2**20
+            collective_id=0, has_side_effects=True, vmem_limit_bytes=48 * 2**20
         ),
         name="snapshot_modes",
-    )(fields, start_local, start_pair, start_root)
+    )(*(pltpu.with_memory_space_constraint(a, pltpu.HBM) for a in (fields, start_local, start_pair, start_root)))
 
 
 def solution(mesh):

time: 82.5 us -> 81.3 us (0.985)
  local copies, waits for them, and re-layouts: 1.77 us -> 0.75 us
    unnamed x1, local copies, waits for them, and re-layouts: 1.77 us -> 0.75 us
where the time goes in v1:
time: 81.3 us; the launch traced here: 81.2 us
  Pallas kernels  80.5 us (99%)
    pallas_call x1, Pallas kernels, on_device(): pl.pallas_call(functools.partial(body, 1.0 / points), out_shape=jax.Shape...  80.5 us

profile of v1, /device:TPU:1, one launch (start us, length us, event | category | flops | bytes accessed | tf_op | source)
XLA Modules:
  0.0 81.2 jit_solution(872979061741844638)
XLA Ops:
  0.0 80.5 %snapshot_modes.1 = bf16[1536,128]{1,0:T(8,128)(2,1)S(1)} custom-call(bf16[6144,256]{1,0:T(8,128)(2,1)} %fields.1, f32[256,128]{1,0:T(8,128)} %start_local.1, f32[2,256,128]{2,1,0:T(8,128)} %start_pair.1, f32[256,128]{1,0:T(8,128)} %start_root.1), custom_call_target="tpu_custom_call" | custom-call | tf_op jit(solution)/shard_map/snapshot_modes/pallas_call | solution.py:350
  80.5 0.7 copy.6

commit v2 on v1

--- a/solution.py
+++ b/solution.py
@@ -15,7 +15,7 @@
 ROW = NY * NC
 SHEET = NZ * NY
 PLANE = NX * ROW
-EARLY = 6
+EARLY = 5
 PIECE = 192
 MESH = pl.DeviceIdType.MESH
 F32 = jnp.float32
@@ -235,23 +235,29 @@
     own_late = pl.ds(pl.multiple_of(x * quarter + early, PIECE), late)
     leaves[x, pl.ds(early, late)] = product(f[own_late], rotation).astype(BF16)
 
+    leaves[x, pl.ds(0, early)] = product(raw[x], rotation).astype(BF16)
     arrived(raw.at[pl.ds(0, NX - 1)], raw_sem)
     arrived(rot_all.at[pl.ds(0, NX - 1)], rot_sem)
-    for b in range(NX):
+    for d in (1, 2, 3):
+        b = lax.rem(x + d, NX)
         leaves[b, pl.ds(0, early)] = product(raw[b], rot_all[b]).astype(BF16)
+
+    def joined(n, rows):
+        return jnp.concatenate([leaves[2 * n, rows], leaves[2 * n + 1, rows]], axis=1)
+
+    first_rows, last_rows, all_rows = slice(0, early), slice(early, quarter), slice(0, quarter)
+    for n in range(2):
+        pair_part[128 * n:128 * n + 128] = product_t(leaves[2 * n, first_rows], leaves[2 * n + 1, first_rows])
     arrived(leaves.at[pl.ds(0, NX - 1), pl.ds(early, late)], leaf_sem)
-
-    pair_part[0:128] = product_t(leaves[0], leaves[1])
-    pair_part[128:256] = product_t(leaves[2], leaves[3])
+    for n in range(2):
+        pair_part[128 * n:128 * n + 128] += product_t(leaves[2 * n, last_rows], leaves[2 * n + 1, last_rows])
 
     @pl.loop(0, PLANE - 1)
     def _(d):
         peer, where = in_plane(d)
         send(pair_part.at[pl.ds(pl.multiple_of(peer * 8, 8), 8)], got_p.at[d], p_sem.at[0], **where)
 
-    left = jnp.concatenate([leaves[0], leaves[1]], axis=1)
-    right = jnp.concatenate([leaves[2], leaves[3]], axis=1)
-    cross_part[...] = product_t(left, right)
+    cross_part[...] = product_t(joined(0, all_rows), joined(1, all_rows))
 
     @pl.loop(0, PLANE - 1)
     def _(d):
@@ -316,7 +322,7 @@
         [jnp.concatenate([first, mixed], axis=1), jnp.concatenate([mixed.T, second], axis=1)], axis=0
     )
     branch = jnp.concatenate(
-        [product(left, rotations[0]).astype(BF16), product(right, rotations[1]).astype(BF16)], axis=1
+        [product(joined(n, all_rows), rotations[n]).astype(BF16) for n in range(2)], axis=1
     )
     bases = [s_root[...].T]
     for _ in range(POWER):

time: 81.3 us -> 79.9 us (0.983)
  Pallas kernels: 80.5 us -> 79.1 us
    pallas_call x1, Pallas kernels: 80.5 us -> 79.1 us  [on_device(): pl.pallas_call(functools.partial(body, 1.0 / points), out_shape=jax.Shape...]
where the time goes in v2:
time: 79.9 us; the launch traced here: 79.8 us
  Pallas kernels  79.1 us (99%)
    pallas_call x1, Pallas kernels, on_device(): pl.pallas_call(functools.partial(body, 1.0 / points), out_shape=jax.Shape...  79.1 us

profile of v2, /device:TPU:1, one launch (start us, length us, event | category | flops | bytes accessed | tf_op | source)
XLA Modules:
  0.0 79.8 jit_solution(16871949041895116360)
XLA Ops:
  0.0 79.1 %snapshot_modes.1 = bf16[1536,128]{1,0:T(8,128)(2,1)S(1)} custom-call(bf16[6144,256]{1,0:T(8,128)(2,1)} %fields.1, f32[256,128]{1,0:T(8,128)} %start_local.1, f32[2,256,128]{2,1,0:T(8,128)} %start_pair.1, f32[256,128]{1,0:T(8,128)} %start_root.1), custom_call_target="tpu_custom_call" | custom-call | tf_op jit(solution)/shard_map/snapshot_modes/pallas_call | solution.py:356
  79.1 0.7 copy.6

commit v3 on v2

--- a/solution.py
+++ b/solution.py
@@ -297,8 +297,9 @@
         arrived(whole_ref.at[pl.ds(0, 8 * (PLANE - 1))], sems.at[2])
 
     over_z(got_p, pair_part, mine_p, zs_p, p_sem)
+    over_z(got_x, cross_part, mine_x, zs_x, x_sem)
     to_plane(zs_p, piece_p, pair_all, p_sem)
-    over_z(got_x, cross_part, mine_x, zs_x, x_sem)
+    to_plane(zs_x, piece_x, cross_all, x_sem)
     arrived(diag_all.at[pl.ds(0, ROW - 1)], g_sem)
     diags = [jnp.concatenate([diag_all[n, b] for n in range(ROW)], axis=0) for b in range(NX)]
     from_plane(pair_all, p_sem)
@@ -311,7 +312,6 @@
 
     grams = [pair_gram(0), pair_gram(1)]
     bases = power_steps(grams, [s_pair[n].T for n in range(2)])
-    to_plane(zs_x, piece_x, cross_all, x_sem)
     bases = power_steps(grams, bases)
     rotations = [basis.T.astype(BF16) for basis in bases]
     first = turned(grams[0], rotations[0], rotations[0])

time: 79.9 us -> 77.2 us (0.966)
  Pallas kernels: 79.1 us -> 76.3 us
    pallas_call x1, Pallas kernels: 79.1 us -> 76.3 us  [on_device(): pl.pallas_call(functools.partial(body, 1.0 / points), out_shape=jax.Shape...]
where the time goes in v3:
time: 77.2 us; the launch traced here: 77.1 us
  Pallas kernels  76.3 us (99%)
    pallas_call x1, Pallas kernels, on_device(): pl.pallas_call(functools.partial(body, 1.0 / points), out_shape=jax.Shape...  76.3 us

profile of v3, /device:TPU:1, one launch (start us, length us, event | category | flops | bytes accessed | tf_op | source)
XLA Modules:
  0.0 77.1 jit_solution(3502471187147873249)
XLA Ops:
  0.0 76.3 %snapshot_modes.1 = bf16[1536,128]{1,0:T(8,128)(2,1)S(1)} custom-call(bf16[6144,256]{1,0:T(8,128)(2,1)} %fields.1, f32[256,128]{1,0:T(8,128)} %start_local.1, f32[2,256,128]{2,1,0:T(8,128)} %start_pair.1, f32[256,128]{1,0:T(8,128)} %start_root.1), custom_call_target="tpu_custom_call" | custom-call | tf_op jit(solution)/shard_map/snapshot_modes/pallas_call | solution.py:356
  76.4 0.7 copy.6

commit v4 on v3

--- a/solution.py
+++ b/solution.py
@@ -111,6 +111,10 @@
         peer, where = in_row(lax.rem(k, ROW))
         return peer_x * ROW + peer, dict(x=peer_x, **where)
 
+    @pl.loop(0, NZ - 1)
+    def _(k):
+        greet(z=away(z, k, NZ), c=1)
+
     loads = []
     for k in range(NX):
         rows = pl.ds(k * quarter, quarter)
@@ -130,10 +134,6 @@
     @pl.when(c == 1)
     def _():
         greet(c=0)
-
-    @pl.loop(0, NZ - 1)
-    def _(k):
-        greet(z=away(z, k, NZ), c=1)
 
     total = None
     for k in range(NX):

time: 77.2 us -> 77.2 us (level)
  no operation moved by 1% of the time
where the time goes in v4:
time: 77.2 us; the launch traced here: 77.1 us
  Pallas kernels  76.4 us (99%)
    pallas_call x1, Pallas kernels, on_device(): pl.pallas_call(functools.partial(body, 1.0 / points), out_shape=jax.Shape...  76.4 us

profile of v4, /device:TPU:1, one launch (start us, length us, event | category | flops | bytes accessed | tf_op | source)
XLA Modules:
  0.0 77.1 jit_solution(13467409314444039888)
XLA Ops:
  0.0 76.4 %snapshot_modes.1 = bf16[1536,128]{1,0:T(8,128)(2,1)S(1)} custom-call(bf16[6144,256]{1,0:T(8,128)(2,1)} %fields.1, f32[256,128]{1,0:T(8,128)} %start_local.1, f32[2,256,128]{2,1,0:T(8,128)} %start_pair.1, f32[256,128]{1,0:T(8,128)} %start_root.1), custom_call_target="tpu_custom_call" | custom-call | tf_op jit(solution)/shard_map/snapshot_modes/pallas_call | solution.py:356
  76.4 0.7 copy.6
